TPU v7x, 128 devices: a whole 4x4x4 slice. The times are simulated.
128 devices in a mesh: seq: 8 (over z, y_hi), chan: 8 (over x, core), dp: 2 (over y_lo).
Axes of the slice: x: 4, y: 4 (y_hi: 2, y_lo: 2; y = y_hi * 2 + y_lo), z: 4, core: 2. Of those that a mesh axis runs over, the one named last changes fastest.
Arguments:
- tokens: bfloat16 [2, 1024, 8192], P('dp', 'seq'), may hold values from -6 to 6
- in_weight: bfloat16 [8192, 3, 4096], P('seq', None, 'chan'), may hold values from -0.0625 to 0.0625
- short_taps: float32 [3, 3, 4096], P(None, None, 'chan'), may hold values from -1 to 1
- long_filter: float32 [1024, 4096], P('seq', 'chan'), may hold values from -1.25 to 1.25
- skip_gain: float32 [4096], P('chan'), may hold values from 0.5 to 1.5
- cotangent: bfloat16 [2, 1024, 4096], P('dp', 'seq', 'chan'), may hold values from -6 to 6
Outputs:
- hyena_out: bfloat16 [2, 1024, 4096], P('dp', 'seq', 'chan')
- grad_tokens: bfloat16 [2, 1024, 8192], P('dp', None, ('seq', 'chan'))
- grad_weight: bfloat16 [8192, 3, 4096], P('seq', None, 'chan')
- grad_filter: float32 [1024, 4096], P('seq', 'chan')
All inputs are finite; a program needn't handle non-finite values.
Results may differ from a plain program's by a relative error of at most 0.02.
Values may be sent and summed in bfloat16 or wider, within the bound.
No kernel may reach another device: no remote copies, remote signals or barrier semaphores. Data moves between devices by JAX's collectives and lax.ppermute only.
A program may use at most 128 MiB of HBM per device.

v0:
```python
import math
import jax
import jax.numpy as jnp
from jax import lax
from jax.sharding import PartitionSpec as P


def partner_2(shard, axis, stride):
    return lax.ppermute(shard, axis, [(i, i ^ 1 << stride) for i in range(lax.axis_size(axis))])


def shifted(value, axis, steps):
    count = lax.axis_size(axis)
    leading, last = (max(0, -steps), min(count, count - steps))
    return lax.ppermute(value, axis, [(source, source + steps) for source in range(leading, last)])


def complex_mul(left, right):
    return jnp.stack(
        [left[0] * right[0] - left[1] * right[1], left[0] * right[1] + left[1] * right[0]]
    )


def conjugate(signal):
    return jnp.stack([signal[0], -signal[1]])


def dft_tables(length):
    index = jnp.arange(length, dtype=jnp.int32)
    product = index[:, None] * index[None, :] % length
    phases = 2.0 * math.pi / length * product.astype(jnp.float32)
    return (jnp.cos(phases), jnp.sin(phases))


def table_apply(cos_table, sin_table, sign, signal, form):
    high = lax.Precision.HIGHEST
    real_cos = jnp.einsum(form, cos_table, signal[0], precision=high)
    imag_cos = jnp.einsum(form, cos_table, signal[1], precision=high)
    real_sin = jnp.einsum(form, sin_table, signal[0], precision=high)
    imag_sin = jnp.einsum(form, sin_table, signal[1], precision=high)
    return jnp.stack([real_cos - sign * imag_sin, imag_cos + sign * real_sin])


def reverse_bits(seq_pos, seq_count):
    bit_total = seq_count.bit_length() - 1
    result = jnp.zeros((), jnp.int32)
    for bit_pos in range(bit_total):
        result = result + seq_pos // (1 << bit_pos) % 2 * (1 << bit_total - 1 - bit_pos)
    return result


def pairs_forward(signal, seq_count, seq_pos):
    bit_total = seq_count.bit_length() - 1
    for bit_pos in reversed(range(bit_total)):
        half_span = 1 << bit_pos
        partner = partner_2(signal, "seq", bit_pos)
        offset = (seq_pos % half_span).astype(jnp.float32)
        phases = -math.pi * offset / half_span
        twiddle = jnp.stack([jnp.cos(phases), jnp.sin(phases)])
        is_upper = seq_pos // half_span % 2 == 1
        signal = jnp.where(is_upper, complex_mul(partner - signal, twiddle), signal + partner)
    return signal


def pairs_inverse(signal, seq_count, seq_pos):
    bit_total = seq_count.bit_length() - 1
    for bit_pos in range(bit_total):
        half_span = 1 << bit_pos
        partner = partner_2(signal.astype(jnp.bfloat16), "seq", bit_pos).astype(signal.dtype)
        offset = (seq_pos % half_span).astype(jnp.float32)
        phases = math.pi * offset / half_span
        twiddle = jnp.stack([jnp.cos(phases), jnp.sin(phases)])
        is_upper = seq_pos // half_span % 2 == 1
        signal = jnp.where(
            is_upper, partner - complex_mul(signal, twiddle), signal + complex_mul(partner, twiddle)
        )
    return signal


def position_twiddle(spec_order, tok_rows, full_len, sign):
    k_index = 2 * spec_order + jnp.arange(2, dtype=jnp.int32)
    pos_rows = jnp.arange(tok_rows, dtype=jnp.int32)
    product = k_index[:, None] * pos_rows[None, :] % full_len
    phases = sign * 2.0 * math.pi / full_len * product.astype(jnp.float32)
    return jnp.stack([jnp.cos(phases), jnp.sin(phases)])[:, None, :, :, None]


def forward_spectrum(rows_in, seq_count, seq_pos):
    tok_rows = rows_in.shape[1]
    full_len = 2 * seq_count * tok_rows
    phase_shift = math.pi * seq_pos.astype(jnp.float32) / seq_count
    real_part = jnp.stack([rows_in, rows_in * jnp.cos(phase_shift)], axis=1)
    imag_part = jnp.stack([jnp.zeros_like(rows_in), -rows_in * jnp.sin(phase_shift)], axis=1)
    signal = jnp.stack([real_part, imag_part])
    signal = pairs_forward(signal, seq_count, seq_pos)
    spec_order = reverse_bits(seq_pos, seq_count)
    signal = complex_mul(signal, position_twiddle(spec_order, tok_rows, full_len, -1.0))
    cos_table, sin_table = dft_tables(tok_rows)
    return table_apply(cos_table, sin_table, -1.0, signal, "ka,gbac->gbkc")


def inverse_spectrum(signal, seq_count, seq_pos):
    tok_rows = signal.shape[3]
    full_len = 2 * seq_count * tok_rows
    cos_table, sin_table = dft_tables(tok_rows)
    signal = table_apply(cos_table, sin_table, 1.0, signal, "ka,gbac->gbkc")
    spec_order = reverse_bits(seq_pos, seq_count)
    signal = complex_mul(signal, position_twiddle(spec_order, tok_rows, full_len, 1.0))
    signal = pairs_inverse(signal, seq_count, seq_pos)
    phase_shift = math.pi * seq_pos.astype(jnp.float32) / seq_count
    combined = (
        signal[0][:, 0]
        + jnp.cos(phase_shift) * signal[0][:, 1]
        - jnp.sin(phase_shift) * signal[1][:, 1]
    )
    return combined / full_len


def local(tokens, in_weight, short_taps, long_filter, skip_gain, cotangent):
    seq_count = lax.axis_size("seq")
    seq_pos = lax.axis_index("seq")
    tok_rows = tokens.shape[1]
    slab_rows = in_weight.shape[0]
    chan_cols = in_weight.shape[2]
    taps_len = short_taps.shape[1]
    grad_scale = 1.0 / math.sqrt(lax.axis_size("dp") * seq_count * tok_rows)
    spread = lax.all_to_all(tokens[0], "seq", split_axis=1, concat_axis=0, tiled=True)
    flat_weight = in_weight.reshape(slab_rows, 3 * chan_cols)
    projected = lax.psum_scatter(
        jnp.dot(spread, flat_weight, preferred_element_type=jnp.float32),
        "seq",
        scatter_dimension=0,
        tiled=True,
    ).reshape(tok_rows, 3, chan_cols)
    rim_rows = shifted(projected[tok_rows - (taps_len - 1) :], "seq", 1)
    extended = jnp.concatenate([rim_rows, projected], axis=0)
    streams = jnp.zeros_like(projected)
    for tap_pos in range(taps_len):
        begin = taps_len - 1 - tap_pos
        streams = streams + short_taps[:, tap_pos, :] * extended[begin : begin + tok_rows]
    queries = streams[:, 0]
    keys_in = streams[:, 1]
    values_in = streams[:, 2]
    gated_in = keys_in * values_in
    spectra = forward_spectrum(jnp.stack([gated_in, long_filter]), seq_count, seq_pos)
    gated_freq = spectra[:, 0:1]
    filter_freq = spectra[:, 1:2]
    conv_out = (
        inverse_spectrum(complex_mul(gated_freq, filter_freq), seq_count, seq_pos)[0]
        + skip_gain * gated_in
    )
    hyena_out = (queries * conv_out).astype(jnp.bfloat16)[None]
    grad_in = cotangent[0].astype(jnp.float32)
    d_conv = grad_in * queries
    d_query = grad_in * conv_out
    conv_freq = forward_spectrum(d_conv[None], seq_count, seq_pos)
    pair_freq = jnp.concatenate(
        [
            complex_mul(conjugate(filter_freq), conv_freq),
            complex_mul(conjugate(gated_freq), conv_freq),
        ],
        axis=1,
    )
    back_rows = inverse_spectrum(pair_freq, seq_count, seq_pos)
    d_gated = back_rows[0] + skip_gain * d_conv
    filter_part = back_rows[1] * grad_scale
    d_streams = jnp.stack([d_query, d_gated * values_in, d_gated * keys_in], axis=1)
    rim_next = shifted(d_streams[: taps_len - 1], "seq", -1)
    ext_next = jnp.concatenate([d_streams, rim_next], axis=0)
    d_projected = jnp.zeros_like(d_streams)
    for tap_pos in range(taps_len):
        d_projected = (
            d_projected + short_taps[:, tap_pos, :] * ext_next[tap_pos : tap_pos + tok_rows]
        )
    d_projected = d_projected.astype(jnp.bfloat16).reshape(tok_rows, 3 * chan_cols)
    shard_rows = lax.all_gather(d_projected, "seq", axis=0, tiled=True)
    weight_total = lax.dot_general(
        spread, shard_rows, (((0,), (0,)), ((), ())), preferred_element_type=jnp.float32
    )
    token_block = lax.dot_general(
        shard_rows, flat_weight, (((1,), (1,)), ((), ())), preferred_element_type=jnp.float32
    )
    grad_tokens = lax.psum_scatter(
        token_block.astype(jnp.bfloat16), "chan", scatter_dimension=1, tiled=True
    )[None]
    weight_sum, filter_sum = (
        lax.psum((weight_total * grad_scale).astype(jnp.bfloat16), "dp").astype(jnp.float32),
        lax.psum(filter_part.astype(jnp.bfloat16), "dp").astype(jnp.float32),
    )
    grad_weight = weight_sum.astype(jnp.bfloat16).reshape(slab_rows, 3, chan_cols)
    return (hyena_out, grad_tokens, grad_weight, filter_sum)


def solution(mesh):
    placed = (
        P("dp", "seq", None),
        P("seq", None, "chan"),
        P(None, None, "chan"),
        P("seq", "chan"),
        P("chan"),
        P("dp", "seq", "chan"),
    )
    return jax.shard_map(
        local,
        mesh=mesh,
        in_specs=placed,
        out_specs=(
            P("dp", "seq", "chan"),
            P("dp", None, ("seq", "chan")),
            P("seq", None, "chan"),
            P("seq", "chan"),
        ),
        check_vma=False,
    )
```

profile of v0, /device:TPU:0, one launch (start us, length us, event | category | flops | bytes accessed | tf_op | source)
XLA Modules:
  0.0 742.5 jit_solution(11029934226150978450)
XLA Ops:
  7.2 4.1 copy.90
  11.3 8.0 %all-to-all-start = ((bf16[128,8,1024]{0,2,1:T(8,128)(2,1)}), bf16[128,8,1024]{0,2,1:T(8,128)(2,1)S(1)}, u32[]{:S(2)}, u32[]{:S(2)}) async-start(bf16[128,8,1024]{0,2,1:T(8,128)(2,1)} %bitcast.318), calls=%async_computation | async-start | bytes 4194304 | tf_op jit(solution)/shard_map/all_to_all | solution.py:127
  19.3 4.6 copy.92
  24.0 23.8 %all-to-all-done = bf16[128,8,1024]{0,2,1:T(8,128)(2,1)S(1)} async-done(((bf16[128,8,1024]{0,2,1:T(8,128)(2,1)}), bf16[128,8,1024]{0,2,1:T(8,128)(2,1)S(1)}, u32[]{:S(2)}, u32[]{:S(2)}) %all-to-all-start) | async-done | bytes 2097184 | tf_op jit(solution)/shard_map/all_to_all | solution.py:127
  47.8 2.6 copy.91
  50.4 8.6 %fusion.204 = f32[1024,1536]{1,0:T(8,128)} fusion(bf16[1024,1024]{1,0:T(8,128)(2,1)} %bitcast.327, bf16[1024,1536]{0,1:T(8,128)(2,1)} %bitcast.323), kind=kOutput, calls=%fused_computation.316 | convolution fusion | flops 3221225472 | bytes 11534336 | tf_op jit(solution)/shard_map/dot_general | solution.py:130
  59.7 95.1 %reduce-scatter.5.cloned.1.call-done = f32[128,1536]{1,0:T(8,128)} async-done(((f32[1024,1536]{1,0:T(8,128)}), f32[128,1536]{1,0:T(8,128)}) %reduce-scatter.5.cloned.1.call-update) | async-done | bytes 786448 | tf_op jit(solution)/shard_map/reduce_scatter | solution.py:129
  155.7 2.4 collective-permute-start
  162.6 4.8 collective-permute-start.1
  167.7 44.0 %collective-permute-done.1 = f32[2,2,2,128,512]{4,3,1,2,0:T(8,128)} collective-permute-done((f32[2,2,2,128,512]{4,3,1,2,0:T(8,128)}, f32[2,2,2,128,512]{4,3,1,2,0:T(8,128)}, u32[]{:S(2)}, u32[]{:S(2)}) %collective-permute-start.1) | collective-permute-done | bytes 2097184 | tf_op jit(solution)/shard_map/ppermute | solution.py:9
  211.6 2.1 fusion.183
  214.0 4.5 maximum_select_fusion
  218.5 2.0 collective-permute-start.2
  220.7 43.1 %collective-permute-done.2 = f32[2,2,2,128,512]{4,3,1,2,0:T(8,128)} collective-permute-done((f32[2,2,2,128,512]{4,3,1,2,0:T(8,128)}, f32[2,2,2,128,512]{4,3,1,2,0:T(8,128)}, u32[]{:S(2)}, u32[]{:S(2)}) %collective-permute-start.2) | collective-permute-done | bytes 2097184 | tf_op jit(solution)/shard_map/ppermute | solution.py:9
  263.8 3.8 fusion.212
  269.1 4.9 maximum_select_fusion.1
  274.0 2.2 collective-permute-start.3
  276.4 43.6 %collective-permute-done.3 = f32[2,2,2,128,512]{4,3,1,2,0:T(8,128)S(1)} collective-permute-done((f32[2,2,2,128,512]{4,3,1,2,0:T(8,128)}, f32[2,2,2,128,512]{4,3,1,2,0:T(8,128)S(1)}, u32[]{:S(2)}, u32[]{:S(2)}) %collective-permute-start.3) | collective-permute-done | bytes 2097184 | tf_op jit(solution)/shard_map/ppermute | solution.py:9
  319.9 2.1 sub.247
  322.2 2.4 maximum_select_fusion.2
  324.9 1.9 fusion.30
  326.9 1.9 fusion.26
  328.8 2.0 fusion.7
  330.8 2.0 fusion.5
  337.0 2.2 collective-permute-start.4
  339.2 8.7 %collective-permute-done.4 = bf16[2,1,2,128,512]{4,3,2,1,0:T(8,128)(2,1)S(1)} collective-permute-done((bf16[2,1,2,128,512]{4,3,2,1,0:T(8,128)(2,1)S(1)}, bf16[2,1,2,128,512]{4,3,2,1,0:T(8,128)(2,1)S(1)}, u32[]{:S(2)}, u32[]{:S(2)}) %collective-permute-start.4) | collective-permute-done | bytes 524320 | tf_op jit(solution)/shard_map/ppermute | solution.py:9
  350.7 8.8 %collective-permute-done.5 = bf16[2,1,2,128,512]{4,3,2,1,0:T(8,128)(2,1)S(1)} collective-permute-done((bf16[2,1,2,128,512]{4,3,2,1,0:T(8,128)(2,1)S(1)}, bf16[2,1,2,128,512]{4,3,2,1,0:T(8,128)(2,1)S(1)}, u32[]{:S(2)}, u32[]{:S(2)}) %collective-permute-start.5) | collective-permute-done | bytes 524320 | tf_op jit(solution)/shard_map/ppermute | solution.py:9
  362.4 10.9 %collective-permute-done.6 = bf16[2,1,2,128,512]{4,3,2,1,0:T(8,128)(2,1)S(1)} collective-permute-done((bf16[2,1,2,128,512]{4,3,2,1,0:T(8,128)(2,1)}, bf16[2,1,2,128,512]{4,3,2,1,0:T(8,128)(2,1)S(1)}, u32[]{:S(2)}, u32[]{:S(2)}) %collective-permute-start.6) | collective-permute-done | bytes 524320 | tf_op jit(solution)/shard_map/ppermute | solution.py:9
  375.9 23.1 %collective-permute-done.7 = f32[2,1,2,128,512]{4,3,2,1,0:T(8,128)S(1)} collective-permute-done((f32[2,1,2,128,512]{4,3,2,1,0:T(8,128)S(1)}, f32[2,1,2,128,512]{4,3,2,1,0:T(8,128)S(1)}, u32[]{:S(2)}, u32[]{:S(2)}) %collective-permute-start.7) | collective-permute-done | bytes 1048608 | tf_op jit(solution)/shard_map/ppermute | solution.py:9
  399.7 2.9 collective-permute-start.8
  402.6 12.8 %collective-permute-done.8 = f32[2,1,2,128,512]{4,3,2,1,0:T(8,128)S(1)} collective-permute-done((f32[2,1,2,128,512]{4,3,2,1,0:T(8,128)S(1)}, f32[2,1,2,128,512]{4,3,2,1,0:T(8,128)S(1)}, u32[]{:S(2)}, u32[]{:S(2)}) %collective-permute-start.8) | collective-permute-done | bytes 1048608 | tf_op jit(solution)/shard_map/ppermute | solution.py:9
  416.7 4.4 collective-permute-start.9
  421.1 12.8 %collective-permute-done.9 = f32[2,1,2,128,512]{4,3,2,1,0:T(8,128)S(1)} collective-permute-done((f32[2,1,2,128,512]{4,3,2,1,0:T(8,128)S(1)}, f32[2,1,2,128,512]{4,3,2,1,0:T(8,128)S(1)}, u32[]{:S(2)}, u32[]{:S(2)}) %collective-permute-start.9) | collective-permute-done | bytes 1048608 | tf_op jit(solution)/shard_map/ppermute | solution.py:9
  446.0 3.8 collective-permute-start.10
  450.0 12.6 %collective-permute-done.10 = bf16[2,2,2,128,512]{4,3,1,2,0:T(8,128)(2,1)S(1)} collective-permute-done((bf16[2,2,2,128,512]{4,3,1,2,0:T(8,128)(2,1)S(1)}, bf16[2,2,2,128,512]{4,3,1,2,0:T(8,128)(2,1)S(1)}, u32[]{:S(2)}, u32[]{:S(2)}) %collective-permute-start.10) | collective-permute-done | bytes 1048608 | tf_op jit(solution)/shard_map/ppermute | solution.py:9
  464.1 2.1 collective-permute-start.11
  466.6 12.4 %collective-permute-done.11 = bf16[2,2,2,128,512]{4,3,1,2,0:T(8,128)(2,1)S(1)} collective-permute-done((bf16[2,2,2,128,512]{4,3,1,2,0:T(8,128)(2,1)S(1)}, bf16[2,2,2,128,512]{4,3,1,2,0:T(8,128)(2,1)S(1)}, u32[]{:S(2)}, u32[]{:S(2)}) %collective-permute-start.11) | collective-permute-done | bytes 1048608 | tf_op jit(solution)/shard_map/ppermute | solution.py:9
  480.5 17.3 %collective-permute-start.12 = (bf16[2,2,2,128,512]{4,3,1,2,0:T(8,128)(2,1)S(1)}, bf16[2,2,2,128,512]{4,3,1,2,0:T(8,128)(2,1)S(1)}, u32[]{:S(2)}, u32[]{:S(2)}) collective-permute-start(bf16[2,2,2,128,512]{4,3,1,2,0:T(8,128)(2,1)S(1)} %get-tuple-element.8), channel_id=1, source_target_pairs={{0,64},{16,80},{32,96},{48,112},{64,0},{80,16},{96,32},{112,48},{1... | collective-permute-start | bytes 3145736 | tf_op jit(solution)/shard_map/ppermute | solution.py:9
  498.2 12.5 %collective-permute-done.12 = bf16[2,2,2,128,512]{4,3,1,2,0:T(8,128)(2,1)S(1)} collective-permute-done((bf16[2,2,2,128,512]{4,3,1,2,0:T(8,128)(2,1)S(1)}, bf16[2,2,2,128,512]{4,3,1,2,0:T(8,128)(2,1)S(1)}, u32[]{:S(2)}, u32[]{:S(2)}) %collective-permute-start.12) | collective-permute-done | bytes 1048608 | tf_op jit(solution)/shard_map/ppermute | solution.py:9
  514.1 5.8 collective-permute-done.13
  521.9 65.9 %all-gather.2.cloned.1.call-done = bf16[1024,1536]{0,1:T(8,128)(2,1)} async-done(((bf16[128,1536]{0,1:T(8,128)(2,1)}), bf16[1024,1536]{0,1:T(8,128)(2,1)}) %all-gather.2.cloned.1.call-update) | async-done | bytes 3145744 | tf_op jit(solution)/shard_map/all_gather | solution.py:176
  587.8 6.8 multiply_convert_fusion
  594.6 4.7 copy.118
  599.6 6.3 convolution_convert_fusion
  605.9 2.6 copy.149
  608.5 84.1 %all-reduce.5.cloned.1.call-done = (bf16[1024,3,512]{2,0,1:T(8,128)(2,1)}, bf16[128,512]{1,0:T(8,128)(2,1)}) async-done(((bf16[1024,3,512]{2,0,1:T(8,128)(2,1)}, bf16[128,512]{1,0:T(8,128)(2,1)}), (bf16[1024,3,512]{2,0,1:T(8,128)(2,1)}, bf16[128,512]{1,0:T(8,128)(2,1)})) %all-reduce.5.cloned.1.call-update) | async-done | bytes 3276816 | tf_op jit(solution)/shard_map/psum | solution.py:187
  694.3 35.9 %reduce-scatter.7.cloned.1.call-done = bf16[128,1024]{1,0:T(8,128)(2,1)} async-done(((bf16[1024,1024]{1,0:T(8,128)(2,1)}), bf16[128,1024]{1,0:T(8,128)(2,1)}) %reduce-scatter.7.cloned.1.call-update) | async-done | bytes 262160
  731.9 3.8 copy.178
  (147 shorter events, 47.4 us)
Async XLA Ops:
  11.3 36.5 %all-to-all-start = ((bf16[128,8,1024]{0,2,1:T(8,128)(2,1)}), bf16[128,8,1024]{0,2,1:T(8,128)(2,1)S(1)}, u32[]{:S(2)}, u32[]{:S(2)}) async-start(bf16[128,8,1024]{0,2,1:T(8,128)(2,1)} %bitcast.318), calls=%async_computation | async-start | bytes 4194304 | tf_op jit(solution)/shard_map/all_to_all | solution.py:127
  19.3 135.6 %reduce-scatter.5.cloned.1.call-start = ((), (), s32[]{:S(2)}) async-start(), calls=%async_computation.3 | async-start | bytes 7077888 | tf_op jit(solution)/shard_map/reduce_scatter | solution.py:129
  59.0 0.7 copy-start.18
  59.0 528.8 %all-gather.2.cloned.1.call-start = ((), (), s32[]{:S(2)}) async-start(), calls=%async_computation.4 | async-start | bytes 3538944 | tf_op jit(solution)/shard_map/all_gather | solution.py:176
  155.7 4.3 collective-permute-start
  158.3 2.0 copy-start.11
  159.7 1.0 copy-start.10
  162.6 49.0 %collective-permute-start.1 = (f32[2,2,2,128,512]{4,3,1,2,0:T(8,128)}, f32[2,2,2,128,512]{4,3,1,2,0:T(8,128)}, u32[]{:S(2)}, u32[]{:S(2)}) collective-permute-start(f32[2,2,2,128,512]{4,3,1,2,0:T(8,128)} %pad_maximum_fusion), channel_id=1, source_target_pairs={{0,64},{16,80},{32,96},{48,112},{64,0},{80,16},{96,32},{112,48},{1... | collective-permute-start | bytes 6291464 | tf_op jit(solution)/shard_map/ppermute | solution.py:9
  214.0 4.5 copy-start
  214.0 4.5 copy-start.2
  218.5 45.3 %collective-permute-start.2 = (f32[2,2,2,128,512]{4,3,1,2,0:T(8,128)}, f32[2,2,2,128,512]{4,3,1,2,0:T(8,128)}, u32[]{:S(2)}, u32[]{:S(2)}) collective-permute-start(f32[2,2,2,128,512]{4,3,1,2,0:T(8,128)} %maximum_select_fusion), channel_id=1, source_target_pairs={{0,32},{16,48},{32,0},{48,16},{64,96},{80,112},{96,64},{112,80},{1... | collective-permute-start | bytes 6291464 | tf_op jit(solution)/shard_map/ppermute | solution.py:9
  267.6 1.2 copy-start.1
  267.6 1.5 copy-start.3
  274.0 45.9 %collective-permute-start.3 = (f32[2,2,2,128,512]{4,3,1,2,0:T(8,128)}, f32[2,2,2,128,512]{4,3,1,2,0:T(8,128)S(1)}, u32[]{:S(2)}, u32[]{:S(2)}) collective-permute-start(f32[2,2,2,128,512]{4,3,1,2,0:T(8,128)} %maximum_select_fusion.1), channel_id=1, source_target_pairs={{0,16},{16,0},{32,48},{48,32},{64,80},{80,64},{96,112},{112,96},{1... | collective-permute-start | bytes 6291464 | tf_op jit(solution)/shard_map/ppermute | solution.py:9
  276.3 48.3 %copy-start.13 = (f32[2,128]{1,0:T(2,128)}, f32[2,128]{1,0:T(2,128)S(1)}, u32[]{:S(2)}) copy-start(f32[2,128]{1,0:T(2,128)S(1)} %get-tuple-element.80) | copy-start | bytes 3076
  276.3 48.3 %copy-start.15 = (f32[2,128]{1,0:T(2,128)}, f32[2,128]{1,0:T(2,128)S(1)}, u32[]{:S(2)}) copy-start(f32[2,128]{1,0:T(2,128)S(1)} %get-tuple-element.81) | copy-start | bytes 3076
  276.3 59.5 %copy-start.19 = (f32[2,128]{1,0:T(2,128)}, f32[2,128]{1,0:T(2,128)S(1)}, u32[]{:S(2)}) copy-start(f32[2,128]{1,0:T(2,128)S(1)} %get-tuple-element.78) | copy-start | bytes 3076
  276.3 59.5 %copy-start.21 = (f32[2,128]{1,0:T(2,128)}, f32[2,128]{1,0:T(2,128)S(1)}, u32[]{:S(2)}) copy-start(f32[2,128]{1,0:T(2,128)S(1)} %get-tuple-element.79) | copy-start | bytes 3076
  330.8 2.1 copy-start.4
  332.8 1.0 copy-start.6
  337.0 11.0 %collective-permute-start.4 = (bf16[2,1,2,128,512]{4,3,2,1,0:T(8,128)(2,1)S(1)}, bf16[2,1,2,128,512]{4,3,2,1,0:T(8,128)(2,1)S(1)}, u32[]{:S(2)}, u32[]{:S(2)}) collective-permute-start(bf16[2,1,2,128,512]{4,3,2,1,0:T(8,128)(2,1)S(1)} %fusion.32), channel_id=1, source_target_pairs={{0,16},{16,0},{32,48},{48,32},{64,80},{80,64},{96,112},{112,96},{1... | collective-permute-start | bytes 1572872 | tf_op jit(solution)/shard_map/ppermute | solution.py:9
  348.7 10.9 %collective-permute-start.5 = (bf16[2,1,2,128,512]{4,3,2,1,0:T(8,128)(2,1)S(1)}, bf16[2,1,2,128,512]{4,3,2,1,0:T(8,128)(2,1)S(1)}, u32[]{:S(2)}, u32[]{:S(2)}) collective-permute-start(bf16[2,1,2,128,512]{4,3,2,1,0:T(8,128)(2,1)S(1)} %get-tuple-element.17), channel_id=1, source_target_pairs={{0,32},{16,48},{32,0},{48,16},{64,96},{80,112},{96,64},{112,80},{1... | collective-permute-start | bytes 1572872 | tf_op jit(solution)/shard_map/ppermute | solution.py:9
  359.8 2.4 copy-start.9
  361.0 12.3 %collective-permute-start.6 = (bf16[2,1,2,128,512]{4,3,2,1,0:T(8,128)(2,1)}, bf16[2,1,2,128,512]{4,3,2,1,0:T(8,128)(2,1)S(1)}, u32[]{:S(2)}, u32[]{:S(2)}) collective-permute-start(bf16[2,1,2,128,512]{4,3,2,1,0:T(8,128)(2,1)} %get-tuple-element.15), channel_id=1, source_target_pairs={{0,64},{16,80},{32,96},{48,112},{64,0},{80,16},{96,32},{112,48},{1... | collective-permute-start | bytes 1572872 | tf_op jit(solution)/shard_map/ppermute | solution.py:9
  374.0 0.7 copy-start.17
  375.8 23.2 %collective-permute-start.7 = (f32[2,1,2,128,512]{4,3,2,1,0:T(8,128)S(1)}, f32[2,1,2,128,512]{4,3,2,1,0:T(8,128)S(1)}, u32[]{:S(2)}, u32[]{:S(2)}) collective-permute-start(f32[2,1,2,128,512]{4,3,2,1,0:T(8,128)S(1)} %pad_maximum_fusion.3), channel_id=1, source_target_pairs={{0,64},{16,80},{32,96},{48,112},{64,0},{80,16},{96,32},{112,48},{1... | collective-permute-start | bytes 3145736 | tf_op jit(solution)/shard_map/ppermute | solution.py:9
  399.7 15.6 %collective-permute-start.8 = (f32[2,1,2,128,512]{4,3,2,1,0:T(8,128)S(1)}, f32[2,1,2,128,512]{4,3,2,1,0:T(8,128)S(1)}, u32[]{:S(2)}, u32[]{:S(2)}) collective-permute-start(f32[2,1,2,128,512]{4,3,2,1,0:T(8,128)S(1)} %maximum_select_fusion.3), channel_id=1, source_target_pairs={{0,32},{16,48},{32,0},{48,16},{64,96},{80,112},{96,64},{112,80},{1... | collective-permute-start | bytes 3145736 | tf_op jit(solution)/shard_map/ppermute | solution.py:9
  416.7 17.2 %collective-permute-start.9 = (f32[2,1,2,128,512]{4,3,2,1,0:T(8,128)S(1)}, f32[2,1,2,128,512]{4,3,2,1,0:T(8,128)S(1)}, u32[]{:S(2)}, u32[]{:S(2)}) collective-permute-start(f32[2,1,2,128,512]{4,3,2,1,0:T(8,128)S(1)} %maximum_select_fusion.4), channel_id=1, source_target_pairs={{0,16},{16,0},{32,48},{48,32},{64,80},{80,64},{96,112},{112,96},{1... | collective-permute-start | bytes 3145736 | tf_op jit(solution)/shard_map/ppermute | solution.py:9
  434.3 0.7 copy-start.14
  434.3 0.7 copy-start.16
  435.0 3.6 copy-start.5
  435.0 3.6 copy-start.7
  442.8 1.3 copy-start.20
  442.8 1.3 copy-start.22
  446.0 16.6 %collective-permute-start.10 = (bf16[2,2,2,128,512]{4,3,1,2,0:T(8,128)(2,1)S(1)}, bf16[2,2,2,128,512]{4,3,1,2,0:T(8,128)(2,1)S(1)}, u32[]{:S(2)}, u32[]{:S(2)}) collective-permute-start(bf16[2,2,2,128,512]{4,3,1,2,0:T(8,128)(2,1)S(1)} %fusion.3), channel_id=1, source_target_pairs={{0,16},{16,0},{32,48},{48,32},{64,80},{80,64},{96,112},{112,96},{1... | collective-permute-start | bytes 3145736 | tf_op jit(solution)/shard_map/ppermute | solution.py:9
  464.1 14.9 %collective-permute-start.11 = (bf16[2,2,2,128,512]{4,3,1,2,0:T(8,128)(2,1)S(1)}, bf16[2,2,2,128,512]{4,3,1,2,0:T(8,128)(2,1)S(1)}, u32[]{:S(2)}, u32[]{:S(2)}) collective-permute-start(bf16[2,2,2,128,512]{4,3,1,2,0:T(8,128)(2,1)S(1)} %get-tuple-element.10), channel_id=1, source_target_pairs={{0,32},{16,48},{32,0},{48,16},{64,96},{80,112},{96,64},{112,80},{1... | collective-permute-start | bytes 3145736 | tf_op jit(solution)/shard_map/ppermute | solution.py:9
  480.5 30.1 %collective-permute-start.12 = (bf16[2,2,2,128,512]{4,3,1,2,0:T(8,128)(2,1)S(1)}, bf16[2,2,2,128,512]{4,3,1,2,0:T(8,128)(2,1)S(1)}, u32[]{:S(2)}, u32[]{:S(2)}) collective-permute-start(bf16[2,2,2,128,512]{4,3,1,2,0:T(8,128)(2,1)S(1)} %get-tuple-element.8), channel_id=1, source_target_pairs={{0,64},{16,80},{32,96},{48,112},{64,0},{80,16},{96,32},{112,48},{1... | collective-permute-start | bytes 3145736 | tf_op jit(solution)/shard_map/ppermute | solution.py:9
  512.6 7.4 copy-start.12
  512.8 7.1 collective-permute-start.13
  519.9 67.8 %copy-start.8 = (bf16[8,128,1024]{2,1,0:T(8,128)(2,1)S(1)}, bf16[8,128,1024]{2,1,0:T(8,128)(2,1)}, u32[]{:S(2)}) copy-start(bf16[8,128,1024]{2,1,0:T(8,128)(2,1)} %copy.91) | copy-start | bytes 6291460
  521.2 171.4 %all-reduce.5.cloned.1.call-start = ((), (), s32[]{:S(2)}) async-start(), calls=%async_computation.6 | async-start | bytes 6553600 | tf_op jit(solution)/shard_map/psum | solution.py:187
  599.3 130.9 %reduce-scatter.7.cloned.1.call-start = ((), (), s32[]{:S(2)}) async-start(), calls=%async_computation.5 | async-start | bytes 2359296
Sparse Core Ops, SparseCore 0:
  59.1 95.7 reduce-scatter.4
  521.3 66.4 all-gather.1
  599.4 93.1 all-reduce.4
  695.6 34.5 reduce-scatter.6
where the time goes:
time: 751 us; the launch traced here: 742 us
  waiting for transfers between devices  556 us (74%)
  starting transfers between devices  56.6 us (8%)
  matrix products  43.9 us (6%)
  other arithmetic  39.1 us (5%)
  local copies, waits for them, and re-layouts  31.3 us (4%)
  between operations  15.8 us (2%)
    ppermute x12, waiting for transfers between devices, partner_2(): lax.ppermute(shard, axis, [(i, i ^ 1 << stride) for i in range(lax.axis_s...  245 us
    reduce_scatter x1, waiting for transfers between devices, local(): lax.psum_scatter(jnp.dot(spread, flat_weight, preferred_element_type=jnp....  95.1 us
    psum x1, waiting for transfers between devices, local(): lax.psum((weight_total * grad_scale).astype(jnp.bfloat16), 'dp')  84.1 us
    all_gather x1, waiting for transfers between devices, local(): shard_rows = lax.all_gather(d_projected, 'seq', axis=0, tiled=True)  65.9 us
    ppermute x12, starting transfers between devices, partner_2(): lax.ppermute(shard, axis, [(i, i ^ 1 << stride) for i in range(lax.axis_s...  44.5 us
    unnamed x5, waiting for transfers between devices  36 us
    all_to_all x1, waiting for transfers between devices, local(): lax.all_to_all(tokens[0], 'seq', split_axis=1, concat_axis=0, tiled=True)  23.8 us
    unnamed x53, local copies, waits for them, and re-layouts  20 us
  transfers between devices with their start and end apart: 19, of which 18 were waited for; matrix products, arithmetic and copies ran while one was open for 3% of the time, Pallas kernels for 0%

commit v1 on v0

--- a/solution.py
+++ b/solution.py
@@ -173,7 +173,9 @@
             d_projected + short_taps[:, tap_pos, :] * ext_next[tap_pos : tap_pos + tok_rows]
         )
     d_projected = d_projected.astype(jnp.bfloat16).reshape(tok_rows, 3 * chan_cols)
-    shard_rows = lax.all_gather(d_projected, "seq", axis=0, tiled=True)
+    shard_rows = jnp.concatenate(
+        lax.all_to_all(jnp.stack(lax.axis_size("seq") * [d_projected], 0), "seq", 0, 0), 0
+    )
     weight_total = lax.dot_general(
         spread, shard_rows, (((0,), (0,)), ((), ())), preferred_element_type=jnp.float32
     )

time: 751 us -> 719 us (0.957)
  waiting for transfers between devices: 556 us -> 513 us
  starting transfers between devices: 56.6 us -> 64.5 us
    all_gather x1 -> x0, waiting for transfers between devices: 65.9 us -> none  [local(): shard_rows = lax.all_gather(d_projected, 'seq', axis=0, tiled=True)]
    all_to_all x0 -> x1, waiting for transfers between devices: none -> 24.1 us  [local(): lax.all_to_all(jnp.stack(lax.axis_size('seq') * [d_projected], 0), 'seq',...]
    all_to_all x0 -> x1, starting transfers between devices: none -> 8.4 us  [local(): lax.all_to_all(jnp.stack(lax.axis_size('seq') * [d_projected], 0), 'seq',...]
    unnamed x53 -> x55, local copies, waits for them, and re-layouts: 20 us -> 17.6 us
    unnamed x5 -> x4, waiting for transfers between devices: 36 us -> 36.1 us
where the time goes in v1:
time: 719 us; the launch traced here: 710 us
  waiting for transfers between devices  513 us (71%)
  starting transfers between devices  64.5 us (9%)
  matrix products  43 us (6%)
  other arithmetic  40.8 us (6%)
  local copies, waits for them, and re-layouts  33.2 us (5%)
  between operations  15.8 us (2%)
    ppermute x12, waiting for transfers between devices, partner_2(): lax.ppermute(shard, axis, [(i, i ^ 1 << stride) for i in range(lax.axis_s...  245 us
    reduce_scatter x1, waiting for transfers between devices, local(): lax.psum_scatter(jnp.dot(spread, flat_weight, preferred_element_type=jnp....  95.1 us
    psum x1, waiting for transfers between devices, local(): lax.psum((weight_total * grad_scale).astype(jnp.bfloat16), 'dp')  81.2 us
    ppermute x12, starting transfers between devices, partner_2(): lax.ppermute(shard, axis, [(i, i ^ 1 << stride) for i in range(lax.axis_s...  43.7 us
    unnamed x4, waiting for transfers between devices  36.1 us
    all_to_all x1, waiting for transfers between devices, local(): lax.all_to_all(tokens[0], 'seq', split_axis=1, concat_axis=0, tiled=True)  25.5 us
    all_to_all x1, waiting for transfers between devices, local(): lax.all_to_all(jnp.stack(lax.axis_size('seq') * [d_projected], 0), 'seq',...  24.1 us
    unnamed x55, local copies, waits for them, and re-layouts  17.6 us
  transfers between devices with their start and end apart: 19, of which 18 were waited for; matrix products, arithmetic and copies ran while one was open for 3% of the time, Pallas kernels for 0%

profile of v1, /device:TPU:0, one launch (start us, length us, event | category | flops | bytes accessed | tf_op | source)
XLA Modules:
  0.0 710.4 jit_solution(11297315026671153554)
XLA Ops:
  7.2 3.2 copy.64
  10.4 2.7 copy.65
  13.1 8.3 %all-to-all-start = ((bf16[128,8,1024]{2,0,1:T(8,128)(2,1)}), bf16[128,8,1024]{2,0,1:T(8,128)(2,1)}, u32[]{:S(2)}, u32[]{:S(2)}) async-start(bf16[128,8,1024]{2,0,1:T(8,128)(2,1)} %copy.65), calls=%async_computation | async-start | bytes 4194304 | tf_op jit(solution)/shard_map/all_to_all | solution.py:127
  21.4 3.0 copy.66
  24.5 25.5 %all-to-all-done = bf16[128,8,1024]{2,0,1:T(8,128)(2,1)} async-done(((bf16[128,8,1024]{2,0,1:T(8,128)(2,1)}), bf16[128,8,1024]{2,0,1:T(8,128)(2,1)}, u32[]{:S(2)}, u32[]{:S(2)}) %all-to-all-start) | async-done | bytes 2097184 | tf_op jit(solution)/shard_map/all_to_all | solution.py:127
  50.0 8.6 %fusion.206 = f32[1024,1536]{1,0:T(8,128)} fusion(bf16[1024,1024]{1,0:T(8,128)(2,1)} %bitcast.2, bf16[1024,1536]{0,1:T(8,128)(2,1)} %bitcast.329), kind=kOutput, calls=%fused_computation.318 | convolution fusion | flops 3221225472 | bytes 11534336 | tf_op jit(solution)/shard_map/dot_general | solution.py:130
  59.3 95.1 %reduce-scatter.5.cloned.1.call-done = f32[128,1536]{1,0:T(8,128)} async-done(((f32[1024,1536]{1,0:T(8,128)}), f32[128,1536]{1,0:T(8,128)}) %reduce-scatter.5.cloned.1.call-update) | async-done | bytes 786448 | tf_op jit(solution)/shard_map/reduce_scatter | solution.py:129
  155.3 2.4 collective-permute-start
  162.2 4.8 collective-permute-start.1
  167.2 44.0 %collective-permute-done.1 = f32[2,2,2,128,512]{4,3,1,2,0:T(8,128)} collective-permute-done((f32[2,2,2,128,512]{4,3,1,2,0:T(8,128)}, f32[2,2,2,128,512]{4,3,1,2,0:T(8,128)}, u32[]{:S(2)}, u32[]{:S(2)}) %collective-permute-start.1) | collective-permute-done | bytes 2097184 | tf_op jit(solution)/shard_map/ppermute | solution.py:9
  211.2 2.1 fusion.185
  213.6 4.5 maximum_select_fusion
  218.1 2.0 collective-permute-start.2
  220.3 43.1 %collective-permute-done.2 = f32[2,2,2,128,512]{4,3,1,2,0:T(8,128)} collective-permute-done((f32[2,2,2,128,512]{4,3,1,2,0:T(8,128)}, f32[2,2,2,128,512]{4,3,1,2,0:T(8,128)}, u32[]{:S(2)}, u32[]{:S(2)}) %collective-permute-start.2) | collective-permute-done | bytes 2097184 | tf_op jit(solution)/shard_map/ppermute | solution.py:9
  263.4 3.8 fusion.213
  268.7 4.9 maximum_select_fusion.1
  273.6 2.2 collective-permute-start.3
  275.9 43.6 %collective-permute-done.3 = f32[2,2,2,128,512]{4,3,1,2,0:T(8,128)S(1)} collective-permute-done((f32[2,2,2,128,512]{4,3,1,2,0:T(8,128)}, f32[2,2,2,128,512]{4,3,1,2,0:T(8,128)S(1)}, u32[]{:S(2)}, u32[]{:S(2)}) %collective-permute-start.3) | collective-permute-done | bytes 2097184 | tf_op jit(solution)/shard_map/ppermute | solution.py:9
  319.5 2.1 sub.247
  321.8 2.4 maximum_select_fusion.2
  330.4 2.0 fusion.7
  336.6 2.2 collective-permute-start.4
  338.8 8.7 %collective-permute-done.4 = bf16[2,1,2,128,512]{4,3,2,1,0:T(8,128)(2,1)S(1)} collective-permute-done((bf16[2,1,2,128,512]{4,3,2,1,0:T(8,128)(2,1)S(1)}, bf16[2,1,2,128,512]{4,3,2,1,0:T(8,128)(2,1)S(1)}, u32[]{:S(2)}, u32[]{:S(2)}) %collective-permute-start.4) | collective-permute-done | bytes 524320 | tf_op jit(solution)/shard_map/ppermute | solution.py:9
  351.0 9.0 %collective-permute-done.5 = bf16[2,1,2,128,512]{4,3,2,1,0:T(8,128)(2,1)S(1)} collective-permute-done((bf16[2,1,2,128,512]{4,3,2,1,0:T(8,128)(2,1)}, bf16[2,1,2,128,512]{4,3,2,1,0:T(8,128)(2,1)S(1)}, u32[]{:S(2)}, u32[]{:S(2)}) %collective-permute-start.5) | collective-permute-done | bytes 524320 | tf_op jit(solution)/shard_map/ppermute | solution.py:9
  362.9 10.9 %collective-permute-done.6 = bf16[2,1,2,128,512]{4,3,2,1,0:T(8,128)(2,1)S(1)} collective-permute-done((bf16[2,1,2,128,512]{4,3,2,1,0:T(8,128)(2,1)}, bf16[2,1,2,128,512]{4,3,2,1,0:T(8,128)(2,1)S(1)}, u32[]{:S(2)}, u32[]{:S(2)}) %collective-permute-start.6) | collective-permute-done | bytes 524320 | tf_op jit(solution)/shard_map/ppermute | solution.py:9
  376.4 23.1 %collective-permute-done.7 = f32[2,1,2,128,512]{4,3,2,1,0:T(8,128)S(1)} collective-permute-done((f32[2,1,2,128,512]{4,3,2,1,0:T(8,128)S(1)}, f32[2,1,2,128,512]{4,3,2,1,0:T(8,128)S(1)}, u32[]{:S(2)}, u32[]{:S(2)}) %collective-permute-start.7) | collective-permute-done | bytes 1048608 | tf_op jit(solution)/shard_map/ppermute | solution.py:9
  400.2 2.9 collective-permute-start.8
  403.1 12.8 %collective-permute-done.8 = f32[2,1,2,128,512]{4,3,2,1,0:T(8,128)S(1)} collective-permute-done((f32[2,1,2,128,512]{4,3,2,1,0:T(8,128)S(1)}, f32[2,1,2,128,512]{4,3,2,1,0:T(8,128)S(1)}, u32[]{:S(2)}, u32[]{:S(2)}) %collective-permute-start.8) | collective-permute-done | bytes 1048608 | tf_op jit(solution)/shard_map/ppermute | solution.py:9
  417.2 5.0 collective-permute-start.9
  422.1 12.8 %collective-permute-done.9 = f32[2,1,2,128,512]{4,3,2,1,0:T(8,128)S(1)} collective-permute-done((f32[2,1,2,128,512]{4,3,2,1,0:T(8,128)S(1)}, f32[2,1,2,128,512]{4,3,2,1,0:T(8,128)S(1)}, u32[]{:S(2)}, u32[]{:S(2)}) %collective-permute-start.9) | collective-permute-done | bytes 1048608 | tf_op jit(solution)/shard_map/ppermute | solution.py:9
  447.0 3.8 collective-permute-start.10
  451.0 12.6 %collective-permute-done.10 = bf16[2,2,2,128,512]{4,3,1,2,0:T(8,128)(2,1)S(1)} collective-permute-done((bf16[2,2,2,128,512]{4,3,1,2,0:T(8,128)(2,1)S(1)}, bf16[2,2,2,128,512]{4,3,1,2,0:T(8,128)(2,1)S(1)}, u32[]{:S(2)}, u32[]{:S(2)}) %collective-permute-start.10) | collective-permute-done | bytes 1048608 | tf_op jit(solution)/shard_map/ppermute | solution.py:9
  465.1 2.1 collective-permute-start.11
  467.6 12.4 %collective-permute-done.11 = bf16[2,2,2,128,512]{4,3,1,2,0:T(8,128)(2,1)S(1)} collective-permute-done((bf16[2,2,2,128,512]{4,3,1,2,0:T(8,128)(2,1)S(1)}, bf16[2,2,2,128,512]{4,3,1,2,0:T(8,128)(2,1)S(1)}, u32[]{:S(2)}, u32[]{:S(2)}) %collective-permute-start.11) | collective-permute-done | bytes 1048608 | tf_op jit(solution)/shard_map/ppermute | solution.py:9
  481.6 16.1 %collective-permute-start.12 = (bf16[2,2,2,128,512]{4,3,1,2,0:T(8,128)(2,1)S(1)}, bf16[2,2,2,128,512]{4,3,1,2,0:T(8,128)(2,1)S(1)}, u32[]{:S(2)}, u32[]{:S(2)}) collective-permute-start(bf16[2,2,2,128,512]{4,3,1,2,0:T(8,128)(2,1)S(1)} %get-tuple-element.8), channel_id=1, source_target_pairs={{0,64},{16,80},{32,96},{48,112},{64,0},{80,16},{96,32},{112,48},{1... | collective-permute-start | bytes 3145736 | tf_op jit(solution)/shard_map/ppermute | solution.py:9
  498.0 12.5 %collective-permute-done.12 = bf16[2,2,2,128,512]{4,3,1,2,0:T(8,128)(2,1)S(1)} collective-permute-done((bf16[2,2,2,128,512]{4,3,1,2,0:T(8,128)(2,1)S(1)}, bf16[2,2,2,128,512]{4,3,1,2,0:T(8,128)(2,1)S(1)}, u32[]{:S(2)}, u32[]{:S(2)}) %collective-permute-start.12) | collective-permute-done | bytes 1048608 | tf_op jit(solution)/shard_map/ppermute | solution.py:9
  513.9 5.8 collective-permute-done.13
  520.3 2.1 stack.271
  522.3 8.4 %all-to-all-start.1 = ((bf16[8,128,1536]{1,2,0:T(8,128)(2,1)}), bf16[8,128,1536]{1,2,0:T(8,128)(2,1)S(1)}, u32[]{:S(2)}, u32[]{:S(2)}) async-start(bf16[8,128,1536]{1,2,0:T(8,128)(2,1)} %stack.271), calls=%async_computation.2 | async-start | bytes 6291456 | tf_op jit(solution)/shard_map/all_to_all | solution.py:177
  532.4 24.1 %all-to-all-done.1 = bf16[8,128,1536]{1,2,0:T(8,128)(2,1)S(1)} async-done(((bf16[8,128,1536]{1,2,0:T(8,128)(2,1)}), bf16[8,128,1536]{1,2,0:T(8,128)(2,1)S(1)}, u32[]{:S(2)}, u32[]{:S(2)}) %all-to-all-start.1) | async-done | bytes 3145760 | tf_op jit(solution)/shard_map/all_to_all | solution.py:177
  556.4 6.0 fusion
  562.5 4.7 copy.93
  567.5 2.8 copy.92
  570.3 6.3 convolution_convert_fusion
  576.6 2.6 copy.124
  579.2 81.2 %all-reduce.5.cloned.1.call-done = (bf16[1024,3,512]{2,0,1:T(8,128)(2,1)}, bf16[128,512]{1,0:T(8,128)(2,1)}) async-done(((bf16[1024,3,512]{2,0,1:T(8,128)(2,1)}, bf16[128,512]{1,0:T(8,128)(2,1)}), (bf16[1024,3,512]{2,0,1:T(8,128)(2,1)}, bf16[128,512]{1,0:T(8,128)(2,1)})) %all-reduce.5.cloned.1.call-update) | async-done | bytes 3276816 | tf_op jit(solution)/shard_map/psum | solution.py:189
  662.0 36.0 %reduce-scatter.7.cloned.1.call-done = bf16[128,1024]{1,0:T(8,128)(2,1)} async-done(((bf16[1024,1024]{1,0:T(8,128)(2,1)}), bf16[128,1024]{1,0:T(8,128)(2,1)}) %reduce-scatter.7.cloned.1.call-update) | async-done | bytes 262160
  699.9 3.8 copy.153
  (150 shorter events, 54.1 us)
Async XLA Ops:
  13.1 8.3 %copy-start.8 = (bf16[1024,3,512]{2,0,1:T(8,128)(2,1)S(1)}, bf16[1024,3,512]{2,0,1:T(8,128)(2,1)}, u32[]{:S(2)}) copy-start(bf16[1024,3,512]{2,0,1:T(8,128)(2,1)} %param.7) | copy-start | bytes 9437188
  13.1 36.9 %all-to-all-start = ((bf16[128,8,1024]{2,0,1:T(8,128)(2,1)}), bf16[128,8,1024]{2,0,1:T(8,128)(2,1)}, u32[]{:S(2)}, u32[]{:S(2)}) async-start(bf16[128,8,1024]{2,0,1:T(8,128)(2,1)} %copy.65), calls=%async_computation | async-start | bytes 4194304 | tf_op jit(solution)/shard_map/all_to_all | solution.py:127
  21.4 133.1 %reduce-scatter.5.cloned.1.call-start = ((), (), s32[]{:S(2)}) async-start(), calls=%async_computation.4 | async-start | bytes 7077888 | tf_op jit(solution)/shard_map/reduce_scatter | solution.py:129
  58.6 0.7 copy-start.19
  155.3 4.3 collective-permute-start
  157.9 2.0 copy-start.12
  159.3 1.0 copy-start.11
  162.2 49.0 %collective-permute-start.1 = (f32[2,2,2,128,512]{4,3,1,2,0:T(8,128)}, f32[2,2,2,128,512]{4,3,1,2,0:T(8,128)}, u32[]{:S(2)}, u32[]{:S(2)}) collective-permute-start(f32[2,2,2,128,512]{4,3,1,2,0:T(8,128)} %pad_maximum_fusion), channel_id=1, source_target_pairs={{0,64},{16,80},{32,96},{48,112},{64,0},{80,16},{96,32},{112,48},{1... | collective-permute-start | bytes 6291464 | tf_op jit(solution)/shard_map/ppermute | solution.py:9
  213.6 4.5 copy-start
  213.6 4.5 copy-start.2
  218.1 45.3 %collective-permute-start.2 = (f32[2,2,2,128,512]{4,3,1,2,0:T(8,128)}, f32[2,2,2,128,512]{4,3,1,2,0:T(8,128)}, u32[]{:S(2)}, u32[]{:S(2)}) collective-permute-start(f32[2,2,2,128,512]{4,3,1,2,0:T(8,128)} %maximum_select_fusion), channel_id=1, source_target_pairs={{0,32},{16,48},{32,0},{48,16},{64,96},{80,112},{96,64},{112,80},{1... | collective-permute-start | bytes 6291464 | tf_op jit(solution)/shard_map/ppermute | solution.py:9
  267.2 1.2 copy-start.1
  267.2 1.5 copy-start.3
  273.6 45.9 %collective-permute-start.3 = (f32[2,2,2,128,512]{4,3,1,2,0:T(8,128)}, f32[2,2,2,128,512]{4,3,1,2,0:T(8,128)S(1)}, u32[]{:S(2)}, u32[]{:S(2)}) collective-permute-start(f32[2,2,2,128,512]{4,3,1,2,0:T(8,128)} %maximum_select_fusion.1), channel_id=1, source_target_pairs={{0,16},{16,0},{32,48},{48,32},{64,80},{80,64},{96,112},{112,96},{1... | collective-permute-start | bytes 6291464 | tf_op jit(solution)/shard_map/ppermute | solution.py:9
  275.9 48.3 %copy-start.14 = (f32[2,128]{1,0:T(2,128)}, f32[2,128]{1,0:T(2,128)S(1)}, u32[]{:S(2)}) copy-start(f32[2,128]{1,0:T(2,128)S(1)} %get-tuple-element.80) | copy-start | bytes 3076
  275.9 48.3 %copy-start.16 = (f32[2,128]{1,0:T(2,128)}, f32[2,128]{1,0:T(2,128)S(1)}, u32[]{:S(2)}) copy-start(f32[2,128]{1,0:T(2,128)S(1)} %get-tuple-element.81) | copy-start | bytes 3076
  275.9 59.5 %copy-start.20 = (f32[2,128]{1,0:T(2,128)}, f32[2,128]{1,0:T(2,128)S(1)}, u32[]{:S(2)}) copy-start(f32[2,128]{1,0:T(2,128)S(1)} %get-tuple-element.78) | copy-start | bytes 3076
  275.9 59.5 %copy-start.22 = (f32[2,128]{1,0:T(2,128)}, f32[2,128]{1,0:T(2,128)S(1)}, u32[]{:S(2)}) copy-start(f32[2,128]{1,0:T(2,128)S(1)} %get-tuple-element.79) | copy-start | bytes 3076
  330.4 2.1 copy-start.4
  332.4 1.0 copy-start.6
  336.6 11.0 %collective-permute-start.4 = (bf16[2,1,2,128,512]{4,3,2,1,0:T(8,128)(2,1)S(1)}, bf16[2,1,2,128,512]{4,3,2,1,0:T(8,128)(2,1)S(1)}, u32[]{:S(2)}, u32[]{:S(2)}) collective-permute-start(bf16[2,1,2,128,512]{4,3,2,1,0:T(8,128)(2,1)S(1)} %fusion.34), channel_id=1, source_target_pairs={{0,16},{16,0},{32,48},{48,32},{64,80},{80,64},{96,112},{112,96},{1... | collective-permute-start | bytes 1572872 | tf_op jit(solution)/shard_map/ppermute | solution.py:9
  349.0 11.0 %collective-permute-start.5 = (bf16[2,1,2,128,512]{4,3,2,1,0:T(8,128)(2,1)}, bf16[2,1,2,128,512]{4,3,2,1,0:T(8,128)(2,1)S(1)}, u32[]{:S(2)}, u32[]{:S(2)}) collective-permute-start(bf16[2,1,2,128,512]{4,3,2,1,0:T(8,128)(2,1)} %get-tuple-element.17), channel_id=1, source_target_pairs={{0,32},{16,48},{32,0},{48,16},{64,96},{80,112},{96,64},{112,80},{1... | collective-permute-start | bytes 1572872 | tf_op jit(solution)/shard_map/ppermute | solution.py:9
  360.3 2.4 copy-start.10
  361.5 12.3 %collective-permute-start.6 = (bf16[2,1,2,128,512]{4,3,2,1,0:T(8,128)(2,1)}, bf16[2,1,2,128,512]{4,3,2,1,0:T(8,128)(2,1)S(1)}, u32[]{:S(2)}, u32[]{:S(2)}) collective-permute-start(bf16[2,1,2,128,512]{4,3,2,1,0:T(8,128)(2,1)} %get-tuple-element.15), channel_id=1, source_target_pairs={{0,64},{16,80},{32,96},{48,112},{64,0},{80,16},{96,32},{112,48},{1... | collective-permute-start | bytes 1572872 | tf_op jit(solution)/shard_map/ppermute | solution.py:9
  374.5 0.7 copy-start.18
  376.3 23.2 %collective-permute-start.7 = (f32[2,1,2,128,512]{4,3,2,1,0:T(8,128)S(1)}, f32[2,1,2,128,512]{4,3,2,1,0:T(8,128)S(1)}, u32[]{:S(2)}, u32[]{:S(2)}) collective-permute-start(f32[2,1,2,128,512]{4,3,2,1,0:T(8,128)S(1)} %pad_maximum_fusion.3), channel_id=1, source_target_pairs={{0,64},{16,80},{32,96},{48,112},{64,0},{80,16},{96,32},{112,48},{1... | collective-permute-start | bytes 3145736 | tf_op jit(solution)/shard_map/ppermute | solution.py:9
  400.2 15.6 %collective-permute-start.8 = (f32[2,1,2,128,512]{4,3,2,1,0:T(8,128)S(1)}, f32[2,1,2,128,512]{4,3,2,1,0:T(8,128)S(1)}, u32[]{:S(2)}, u32[]{:S(2)}) collective-permute-start(f32[2,1,2,128,512]{4,3,2,1,0:T(8,128)S(1)} %maximum_select_fusion.3), channel_id=1, source_target_pairs={{0,32},{16,48},{32,0},{48,16},{64,96},{80,112},{96,64},{112,80},{1... | collective-permute-start | bytes 3145736 | tf_op jit(solution)/shard_map/ppermute | solution.py:9
  417.2 17.7 %collective-permute-start.9 = (f32[2,1,2,128,512]{4,3,2,1,0:T(8,128)S(1)}, f32[2,1,2,128,512]{4,3,2,1,0:T(8,128)S(1)}, u32[]{:S(2)}, u32[]{:S(2)}) collective-permute-start(f32[2,1,2,128,512]{4,3,2,1,0:T(8,128)S(1)} %maximum_select_fusion.4), channel_id=1, source_target_pairs={{0,16},{16,0},{32,48},{48,32},{64,80},{80,64},{96,112},{112,96},{1... | collective-permute-start | bytes 3145736 | tf_op jit(solution)/shard_map/ppermute | solution.py:9
  435.3 0.7 copy-start.15
  435.3 0.7 copy-start.17
  436.0 3.6 copy-start.5
  436.0 3.6 copy-start.7
  443.8 1.3 copy-start.21
  443.8 1.3 copy-start.23
  447.0 16.6 %collective-permute-start.10 = (bf16[2,2,2,128,512]{4,3,1,2,0:T(8,128)(2,1)S(1)}, bf16[2,2,2,128,512]{4,3,1,2,0:T(8,128)(2,1)S(1)}, u32[]{:S(2)}, u32[]{:S(2)}) collective-permute-start(bf16[2,2,2,128,512]{4,3,1,2,0:T(8,128)(2,1)S(1)} %fusion.5), channel_id=1, source_target_pairs={{0,16},{16,0},{32,48},{48,32},{64,80},{80,64},{96,112},{112,96},{1... | collective-permute-start | bytes 3145736 | tf_op jit(solution)/shard_map/ppermute | solution.py:9
  465.1 14.9 %collective-permute-start.11 = (bf16[2,2,2,128,512]{4,3,1,2,0:T(8,128)(2,1)S(1)}, bf16[2,2,2,128,512]{4,3,1,2,0:T(8,128)(2,1)S(1)}, u32[]{:S(2)}, u32[]{:S(2)}) collective-permute-start(bf16[2,2,2,128,512]{4,3,1,2,0:T(8,128)(2,1)S(1)} %get-tuple-element.10), channel_id=1, source_target_pairs={{0,32},{16,48},{32,0},{48,16},{64,96},{80,112},{96,64},{112,80},{1... | collective-permute-start | bytes 3145736 | tf_op jit(solution)/shard_map/ppermute | solution.py:9
  481.6 28.9 %collective-permute-start.12 = (bf16[2,2,2,128,512]{4,3,1,2,0:T(8,128)(2,1)S(1)}, bf16[2,2,2,128,512]{4,3,1,2,0:T(8,128)(2,1)S(1)}, u32[]{:S(2)}, u32[]{:S(2)}) collective-permute-start(bf16[2,2,2,128,512]{4,3,1,2,0:T(8,128)(2,1)S(1)} %get-tuple-element.8), channel_id=1, source_target_pairs={{0,64},{16,80},{32,96},{48,112},{64,0},{80,16},{96,32},{112,48},{1... | collective-permute-start | bytes 3145736 | tf_op jit(solution)/shard_map/ppermute | solution.py:9
  512.4 1.5 copy-start.9
  512.4 7.4 %copy-start.13 = (f32[3,1,512]{2,0,1:T(4,128)S(1)}, f32[3,1,512]{2,0,1:T(4,128)}, u32[]{:S(2)}) copy-start(f32[3,1,512]{2,0,1:T(4,128)} %copy-done.12) | copy-start | bytes 18436
  512.6 7.1 collective-permute-start.13
  522.3 34.1 %all-to-all-start.1 = ((bf16[8,128,1536]{1,2,0:T(8,128)(2,1)}), bf16[8,128,1536]{1,2,0:T(8,128)(2,1)S(1)}, u32[]{:S(2)}, u32[]{:S(2)}) async-start(bf16[8,128,1536]{1,2,0:T(8,128)(2,1)} %stack.271), calls=%async_computation.2 | async-start | bytes 6291456 | tf_op jit(solution)/shard_map/all_to_all | solution.py:177
  530.7 129.7 %all-reduce.5.cloned.1.call-start = ((), (), s32[]{:S(2)}) async-start(), calls=%async_computation.6 | async-start | bytes 6553600 | tf_op jit(solution)/shard_map/psum | solution.py:189
  567.2 130.9 %reduce-scatter.7.cloned.1.call-start = ((), (), s32[]{:S(2)}) async-start(), calls=%async_computation.5 | async-start | bytes 2359296
Sparse Core Ops, SparseCore 0:
  58.7 95.7 reduce-scatter.4
  567.3 93.0 all-reduce.4
  663.5 34.5 reduce-scatter.6
